TPU v7x, 32 devices: a whole 2x2x4 slice. The times are simulated.
32 devices in a mesh: dp: 4 (over z), ctx: 8 (over y, x, core).
Axes of the slice: x: 2, y: 2, z: 4, core: 2. Of those that a mesh axis runs over, the one named last changes fastest.
Arguments:
- inputs: bfloat16 [4, 2048, 4096], P('dp', 'ctx'), may hold values from -6 to 6
- value_weight: bfloat16 [4096, 512], P('ctx'), may hold values from -0.09375 to 0.09375
- query_states: bfloat16 [4, 2048, 2048], P('dp', 'ctx'), may hold values from -40 to 40
- key_states: bfloat16 [4, 2048, 512], P('dp', 'ctx'), may hold values from -6 to 6
- value_states: bfloat16 [4, 2048, 512], P('dp', 'ctx'), may hold values from -6 to 6
- attention_out: bfloat16 [4, 2048, 2048], P('dp', 'ctx'), may hold values from -4 to 4
- out_grad: bfloat16 [4, 2048, 2048], P('dp', 'ctx'), may hold values from -6 to 6
- segment_ids: int32 [4, 2048], P('dp', 'ctx'), may hold values from 0 to 3, never falling along the last dimension, each value on 1 to 1024 neighbouring positions
Outputs:
- query_grad: bfloat16 [4, 2048, 2048], P('dp', 'ctx')
- key_grad: bfloat16 [4, 2048, 512], P('dp', 'ctx')
- input_grad: bfloat16 [4, 2048, 4096], P('dp', 'ctx')
- weight_grad: float32 [4096, 512], P('ctx')
Inputs may be any that keep to these rules, and one draw needn't show every extreme that they name: `segment_ids`: along each sequence the ids never fall; each record holds 1 to 1024 tokens and one holds exactly 1024.
All inputs are finite; a program needn't handle non-finite values.
Results may differ from a plain program's by a relative error of at most 0.0057.
Values may be sent and summed in bfloat16 or wider, within the bound.
No kernel may reach another device: no remote copies, remote signals or barrier semaphores. Data moves between devices by JAX's collectives and lax.ppermute only.
A program may use at most 128 MiB of HBM per device.

v0:
```python
import math
import jax
import jax.numpy as jnp
from jax import lax
from jax.sharding import PartitionSpec as P

HQ = 16
KVH = 4
DH = 128
W = 2048


def carried_in(value, axis, combine, identity):
    peers, here = (lax.axis_size(axis), lax.axis_index(axis))
    everything = jax.tree.map(lambda part: lax.all_gather(part, axis), value)
    start = jax.tree.map(
        lambda part, zero: jnp.broadcast_to(jnp.asarray(zero, part.dtype), part.shape),
        value,
        identity,
    )

    def turn(k, before):
        reached = k < here
        new = combine(before, jax.tree.map(lambda part: part[k], everything))
        return jax.tree.map(lambda a, b: jnp.where(reached, a, b), new, before)

    return lax.fori_loop(0, peers, turn, start)


def passed_along(block, axis, distance):
    devices = range(lax.axis_size(axis))
    route = [(i - distance, i) for i in devices if i - distance in devices]
    return lax.ppermute(block, axis, route)


def link_records(earlier, later):
    first_early, last_early, start_early, whole_early, empty_early = earlier
    first_late, last_late, start_late, whole_late, empty_late = later
    joined = last_early == first_late
    start_merged = jnp.where((whole_late == 1) & joined, start_early, start_late)
    whole_merged = jnp.where((whole_early == 1) & (whole_late == 1) & joined, 1, 0).astype(
        jnp.int32
    )
    merged = (first_early, last_late, start_merged, whole_merged, jnp.zeros_like(empty_early))
    return tuple(
        (
            jnp.where(
                empty_early == 1, late_item, jnp.where(empty_late == 1, early_item, merged_item)
            )
            for early_item, late_item, merged_item in zip(earlier, later, merged)
        )
    )


def attend_group(operands, live_mask, factor):
    query_group, key_group, value_group, grad_group, output_group = operands
    scores = (
        jnp.einsum("gqd,kd->gqk", query_group, key_group, preferred_element_type=jnp.float32)
        * factor
    )
    scores = jnp.where(live_mask[None], scores, -1e30)
    row_max = jnp.max(scores, axis=-1, keepdims=True)
    exp_score = jnp.exp(scores - row_max)
    prob_full = exp_score / jnp.sum(exp_score, axis=-1, keepdims=True)
    prob_low = prob_full.astype(jnp.bfloat16)
    row_delta = jnp.sum(
        grad_group.astype(jnp.float32) * output_group.astype(jnp.float32), axis=-1, keepdims=True
    )
    prob_grad = jnp.einsum(
        "gqd,kd->gqk", grad_group, value_group, preferred_element_type=jnp.float32
    )
    score_grad = (prob_full * (prob_grad - row_delta)).astype(jnp.bfloat16)
    query_part = (
        jnp.einsum("gqk,kd->gqd", score_grad, key_group, preferred_element_type=jnp.float32)
        * factor
    )
    key_part = (
        jnp.einsum("gqk,gqd->kd", score_grad, query_group, preferred_element_type=jnp.float32)
        * factor
    )
    value_part = jnp.einsum("gqk,gqd->kd", prob_low, grad_group, preferred_element_type=jnp.float32)
    return (query_part, key_part, value_part)


def attend_tail(factor, operands):
    query_heads, key_heads, value_heads, grad_heads, output_heads, live_mask = operands
    query_part, key_part, value_part = lax.map(
        lambda head_parts: attend_group(head_parts, live_mask, factor),
        (query_heads, key_heads, value_heads, grad_heads, output_heads),
    )
    return (query_part, key_part, value_part)


def on_device(
    inputs,
    value_weight,
    query_states,
    key_states,
    value_states,
    attention_out,
    out_grad,
    segment_ids,
):
    tok_rows = query_states.shape[1]
    span_blocks = W // tok_rows
    group_size = HQ // KVH
    width_kv = KVH * DH
    factor = 1.0 / math.sqrt(DH)
    window_rows = (span_blocks + 1) * tok_rows
    input_rows = inputs[0]
    values = value_states[0]
    seg_local = segment_ids[0]
    device_index = lax.axis_index("ctx")
    offset = device_index * tok_rows
    before = jnp.sum((seg_local[None, :] < seg_local[:, None]).astype(jnp.int32), axis=1)
    first_id = seg_local[0]
    last_id = seg_local[-1]
    summary = (
        first_id,
        last_id,
        offset + before[-1],
        (first_id == last_id).astype(jnp.int32),
        jnp.zeros((), jnp.int32),
    )
    identity = tuple((jnp.full((), filler, jnp.int32) for filler in (0, 0, 0, 1, 1)))
    prior = carried_in(summary, "ctx", link_records, identity)
    carried = (before == 0) & (prior[4] == 0) & (prior[1] == first_id)
    starts = jnp.where(carried, prior[2], offset + before)
    kv_block = jnp.stack([key_states[0], values])
    doubling_plan = []
    window = kv_block
    blocks_held = 1
    while blocks_held < span_blocks + 1:
        needed = min(blocks_held, span_blocks + 1 - blocks_held)
        received = passed_along(window[:, (blocks_held - needed) * tok_rows :], "ctx", blocks_held)
        window = jnp.concatenate([received, window], axis=1)
        doubling_plan.append((blocks_held, needed))
        blocks_held = blocks_held + needed
    key_base = offset - span_blocks * tok_rows
    key_pos = key_base + jnp.arange(window_rows, dtype=jnp.int32)
    query_pos = offset + jnp.arange(tok_rows, dtype=jnp.int32)
    live_mask = (
        (key_pos[None, :] >= starts[:, None])
        & (key_pos[None, :] <= query_pos[:, None])
        & (key_pos[None, :] > query_pos[:, None] - W)
    )
    query_heads = query_states[0].reshape(tok_rows, KVH, group_size, DH).transpose(1, 2, 0, 3)
    grad_heads = out_grad[0].reshape(tok_rows, KVH, group_size, DH).transpose(1, 2, 0, 3)
    output_heads = attention_out[0].reshape(tok_rows, KVH, group_size, DH).transpose(1, 2, 0, 3)
    key_heads = window[0].reshape(window_rows, KVH, DH).transpose(1, 0, 2)
    value_heads = window[1].reshape(window_rows, KVH, DH).transpose(1, 0, 2)
    operands = (query_heads, key_heads, value_heads, grad_heads, output_heads, live_mask)
    query_part, key_part, value_part = attend_tail(factor, operands)
    query_grad = query_part.transpose(2, 0, 1, 3).reshape(1, tok_rows, HQ * DH).astype(jnp.bfloat16)
    grads = jnp.stack(
        [
            key_part.transpose(1, 0, 2).reshape(window_rows, width_kv),
            value_part.transpose(1, 0, 2).reshape(window_rows, width_kv),
        ]
    )
    for blocks_held, needed in reversed(doubling_plan):
        sent = grads[:, : needed * tok_rows]
        kept_rows = grads[:, needed * tok_rows :]
        returned = passed_along(sent, "ctx", -blocks_held)
        split_at = (blocks_held - needed) * tok_rows
        grads = jnp.concatenate(
            [kept_rows[:, :split_at], kept_rows[:, split_at:] + returned], axis=1
        )
    key_grad = grads[0].astype(jnp.bfloat16)[None]
    value_delta = grads[1].astype(jnp.bfloat16)
    input_grad = jnp.einsum(
        "tk,rk->tr",
        value_delta,
        lax.all_gather(value_weight, "ctx", axis=0, tiled=True),
        preferred_element_type=jnp.float32,
    )
    input_grad = input_grad.astype(jnp.bfloat16)[None]
    weight_share = lax.psum_scatter(
        jnp.einsum("tr,tk->rk", input_rows, value_delta, preferred_element_type=jnp.float32),
        "ctx",
        scatter_dimension=0,
        tiled=True,
    )
    weight_grad = lax.psum(weight_share, "dp")
    return (query_grad, key_grad, input_grad, weight_grad)


def solution(mesh):
    placed = (
        P("dp", "ctx", None),
        P("ctx", None),
        P("dp", "ctx", None),
        P("dp", "ctx", None),
        P("dp", "ctx", None),
        P("dp", "ctx", None),
        P("dp", "ctx", None),
        P("dp", "ctx"),
    )
    return jax.shard_map(
        on_device,
        mesh=mesh,
        in_specs=placed,
        out_specs=(
            P("dp", "ctx", None),
            P("dp", "ctx", None),
            P("dp", "ctx", None),
            P("ctx", None),
        ),
        check_vma=False,
    )
```

profile of v0, /device:TPU:0, one launch (start us, length us, event | category | flops | bytes accessed | tf_op | source)
XLA Modules:
  0.0 681.1 jit_solution(11382272146703181672)
XLA Ops:
  10.4 2.4 collective-permute-start.1
  14.6 11.5 %collective-permute-start.2 = (bf16[2,512,512]{1,2,0:T(8,128)(2,1)S(1)}, bf16[2,512,512]{1,2,0:T(8,128)(2,1)S(1)}, u32[]{:S(2)}, u32[]{:S(2)}) collective-permute-start(bf16[2,512,512]{1,2,0:T(8,128)(2,1)S(1)} %maximum_maximum_fusion.1), channel_id=1, source_target_pairs={{0,2},{1,3},{2,4},{3,5},{4,6},{5,7},{8,10},{9,11},{10,12},{11,13},... | collective-permute-start | bytes 3145736 | tf_op jit(solution)/shard_map/ppermute | solution.py:33
  26.1 21.7 %collective-permute-done.2 = bf16[2,512,512]{1,2,0:T(8,128)(2,1)S(1)} collective-permute-done((bf16[2,512,512]{1,2,0:T(8,128)(2,1)S(1)}, bf16[2,512,512]{1,2,0:T(8,128)(2,1)S(1)}, u32[]{:S(2)}, u32[]{:S(2)}) %collective-permute-start.2) | collective-permute-done | bytes 1048608 | tf_op jit(solution)/shard_map/ppermute | solution.py:33
  50.5 6.7 collective-permute-start.3
  67.4 31.2 %all-reduce.5 = (s32[8]{0:T(128)S(1)}, s32[8]{0:T(128)S(1)}, s32[8]{0:T(128)S(1)}, s32[8]{0:T(128)S(1)}, s32[8]{0:T(128)S(1)}) all-reduce(s32[8]{0:T(128)S(1)} %bitcast_dynamic-update-slice_fusion.1, s32[8]{0:T(128)S(1)} %dynamic-update-slice.1, s32[8]{0:T(128)S(1)} %dynamic-update-slice.2, ...), channel_id=2, replica_groups=mesh['dp'=4,'ctx'=8] {'ctx'}, use_global_device_ids=true, to_apply=%add | all-reduce | flops 40 | bytes 320 | tf_op jit(solution)/shard_map/all_gather | solution.py:15
  98.6 66.3 %while.32 = (s32[]{:T(128)}, s32[]{:T(128)}, s32[]{:T(128)}, s32[]{:T(128)}, s32[]{:T(128)}, /*index=5*/s32[8]{0:T(128)S(1)}, s32[8]{0:T(128)S(1)}, s32[8]{0:T(1...) while((s32[]{:T(128)}, s32[]{:T(128)}, s32[]{:T(128)}, s32[]{:T(128)}, ...), condition=%wide.region_2.3_spmd, body=%wide.region_1.2_spmd.sunk | while | flops 18 | bytes 363 | solution.py:27
  165.6 2.3 copy.39
  167.9 2.3 copy.40
  170.1 2.3 copy.36
  175.6 2.5 fusion.83
  178.1 120.7 %while.33 = (s32[]{:T(128)}, bf16[4,4,256,128]{3,2,1,0:T(8,128)(2,1)}, f32[4,2304,128]{2,1,0:T(8,128)}, f32[4,2304,128]{2,1,0:T(8,128)}, bf16[4,4,256,128]{2,3,1...) while((s32[]{:T(128)}, ...), condition=%wide.region_7.8_spmd.clone, body=%wide.region_3.7_spmd.clone.sunk | while | flops 3658453504 | bytes 52402368 | solution.py:87
  180.5 8.4 %fusion.118 = (f32[4,256]{1,0:T(4,128)S(1)}, f32[4,256,2304]{2,1,0:T(8,128)}) fusion(pred[256,2304]{1,0:T(8,128)(4,1)S(1)} %compare_and_fusion.2, bf16[4,2304,128]{1,2,0:T(8,128)(2,1)} %get-tuple-element.586, s32[]{:T(128)} %get-tuple-element.567, bf16[4,4,256,128]{2,3,1,0:T(8,128)(2,1)} %get-tuple-element.585), kind=kOutput, calls=%fused_computation.87.clone.1 | convolution fusion | flops 613419264 | bytes 10884096 | tf_op jit(solution)/shard_map/while/body/eval_jaxpr/sub | solution.py:63
  188.9 5.4 multiply_convert_fusion.2
  194.4 3.5 fusion.120
  197.9 2.5 fusion.119
  201.4 6.8 fusion.121
  210.7 8.4 %fusion.118 = (f32[4,256]{1,0:T(4,128)S(1)}, f32[4,256,2304]{2,1,0:T(8,128)}) fusion(pred[256,2304]{1,0:T(8,128)(4,1)S(1)} %compare_and_fusion.2, bf16[4,2304,128]{1,2,0:T(8,128)(2,1)} %get-tuple-element.586, s32[]{:T(128)} %get-tuple-element.567, bf16[4,4,256,128]{2,3,1,0:T(8,128)(2,1)} %get-tuple-element.585), kind=kOutput, calls=%fused_computation.87.clone.1 | convolution fusion | flops 613419264 | bytes 10884096 | tf_op jit(solution)/shard_map/while/body/eval_jaxpr/sub | solution.py:63
  219.1 5.4 multiply_convert_fusion.2
  224.5 3.5 fusion.120
  228.0 2.5 fusion.119
  231.5 6.8 %fusion.121 = f32[4,2304,128]{2,1,0:T(8,128)} fusion(f32[4,2304,128]{2,1,0:T(8,128)} %get-tuple-element.570, s32[]{:T(128)} %get-tuple-element.567, f32[4,256]{1,0:T(4,128)S(1)} %get-tuple-element.513, pred[256,2304]{1,0:T(8,128)(4,1)S(1)} %compare_and_fusion.2, bf16[4,2304,128]{1,2,0:T(8,128)(2,1)} %get-tuple-element.586, ...), kind=kOutput, calls=%fused_computation.17.clone.1 | convolution fusion | flops 1219759360 | bytes 2889728 | tf_op jit(solution)/shard_map/while/body/eval_jaxpr/gqk,gqd->kd/dot_general | solution.py:81
  240.8 8.4 %fusion.118 = (f32[4,256]{1,0:T(4,128)S(1)}, f32[4,256,2304]{2,1,0:T(8,128)}) fusion(pred[256,2304]{1,0:T(8,128)(4,1)S(1)} %compare_and_fusion.2, bf16[4,2304,128]{1,2,0:T(8,128)(2,1)} %get-tuple-element.586, s32[]{:T(128)} %get-tuple-element.567, bf16[4,4,256,128]{2,3,1,0:T(8,128)(2,1)} %get-tuple-element.585), kind=kOutput, calls=%fused_computation.87.clone.1 | convolution fusion | flops 613419264 | bytes 10884096 | tf_op jit(solution)/shard_map/while/body/eval_jaxpr/sub | solution.py:63
  249.2 5.4 multiply_convert_fusion.2
  254.7 3.6 fusion.120
  258.2 2.5 fusion.119
  261.8 6.8 fusion.121
  271.0 8.4 %fusion.118 = (f32[4,256]{1,0:T(4,128)S(1)}, f32[4,256,2304]{2,1,0:T(8,128)}) fusion(pred[256,2304]{1,0:T(8,128)(4,1)S(1)} %compare_and_fusion.2, bf16[4,2304,128]{1,2,0:T(8,128)(2,1)} %get-tuple-element.586, s32[]{:T(128)} %get-tuple-element.567, bf16[4,4,256,128]{2,3,1,0:T(8,128)(2,1)} %get-tuple-element.585), kind=kOutput, calls=%fused_computation.87.clone.1 | convolution fusion | flops 613419264 | bytes 10884096 | tf_op jit(solution)/shard_map/while/body/eval_jaxpr/sub | solution.py:63
  279.4 5.4 multiply_convert_fusion.2
  284.9 3.5 fusion.120
  288.4 2.5 fusion.119
  291.9 6.8 %fusion.121 = f32[4,2304,128]{2,1,0:T(8,128)} fusion(f32[4,2304,128]{2,1,0:T(8,128)} %get-tuple-element.570, s32[]{:T(128)} %get-tuple-element.567, f32[4,256]{1,0:T(4,128)S(1)} %get-tuple-element.513, pred[256,2304]{1,0:T(8,128)(4,1)S(1)} %compare_and_fusion.2, bf16[4,2304,128]{1,2,0:T(8,128)(2,1)} %get-tuple-element.586, ...), kind=kOutput, calls=%fused_computation.17.clone.1 | convolution fusion | flops 1219759360 | bytes 2889728 | tf_op jit(solution)/shard_map/while/body/eval_jaxpr/gqk,gqd->kd/dot_general | solution.py:81
  298.7 11.1 %copy.47 = f32[2304,4,128]{2,1,0:T(4,128)} copy(f32[2304,4,128]{2,0,1:T(8,128)} %bitcast.169) | data formatting | bytes 9437184 | tf_op jit(solution)/shard_map/transpose | solution.py:157
  309.8 6.6 stack_reshape.6
  316.4 5.2 constant_dynamic-update-slice_fusion.6
  321.6 10.9 %copy.48 = f32[2304,4,128]{2,1,0:T(4,128)} copy(f32[2304,4,128]{2,0,1:T(8,128)S(1)} %bitcast.172) | data formatting | bytes 9437184 | tf_op jit(solution)/shard_map/transpose | solution.py:158
  332.5 6.5 stack_reshape.7
  339.1 5.0 constant_dynamic-update-slice_fusion.5
  344.1 2.8 slice.82
  351.8 86.6 %collective-permute-done.5 = f32[2,1024,512]{2,1,0:T(8,128)} collective-permute-done((f32[2,1024,512]{2,1,0:T(8,128)S(1)}, f32[2,1024,512]{2,1,0:T(8,128)}, u32[]{:S(2)}, u32[]{:S(2)}) %collective-permute-start.5) | collective-permute-done | bytes 4194336 | tf_op jit(solution)/shard_map/ppermute | solution.py:33
  438.4 3.2 fusion.73
  443.1 43.9 %collective-permute-done.6 = f32[2,512,512]{2,1,0:T(8,128)S(1)} collective-permute-done((f32[2,512,512]{2,1,0:T(8,128)S(1)}, f32[2,512,512]{2,1,0:T(8,128)S(1)}, u32[]{:S(2)}, u32[]{:S(2)}) %collective-permute-start.6) | collective-permute-done | bytes 2097184 | tf_op jit(solution)/shard_map/ppermute | solution.py:33
  488.9 3.3 collective-permute-done.7
  493.3 4.5 convolution_bitcast_fusion.1
  498.6 80.7 %reduce-scatter.2.cloned.1.call-done = f32[512,512]{0,1:T(8,128)} async-done(((f32[4096,512]{0,1:T(8,128)}), f32[512,512]{0,1:T(8,128)}) %reduce-scatter.2.cloned.1.call-update) | async-done | bytes 1048592 | tf_op jit(solution)/shard_map/reduce_scatter | solution.py:178
  584.6 33.2 %all-gather.4.cloned.1.call-done = bf16[4096,512]{1,0:T(8,128)(2,1)} async-done(((bf16[512,512]{1,0:T(8,128)(2,1)}), bf16[4096,512]{1,0:T(8,128)(2,1)}) %all-gather.4.cloned.1.call-update) | async-done | bytes 4194320 | tf_op jit(solution)/shard_map/all_gather | solution.py:174
  617.8 4.9 fusion.72
  622.7 49.4 %all-reduce.8.cloned.1.call-done = f32[512,512]{0,1:T(8,128)} async-done(((f32[512,512]{0,1:T(8,128)}), f32[512,512]{0,1:T(8,128)}) %all-reduce.8.cloned.1.call-update) | async-done | bytes 1048592 | tf_op jit(solution)/shard_map/psum | solution.py:184
  672.1 2.5 copy.49
  (150 shorter events, 73.6 us)
Async XLA Ops:
  7.2 486.1 %copy-start = (bf16[1,256,4096]{2,1,0:T(8,128)(2,1)S(1)}, bf16[1,256,4096]{2,1,0:T(8,128)(2,1)}, u32[]{:S(2)}) copy-start(bf16[1,256,4096]{2,1,0:T(8,128)(2,1)} %param.12) | copy-start | bytes 6291460
  7.2 54.1 %copy-start.8 = (u32[32]{0:T(128)S(1)}, u32[32]{0:T(128)}, u32[]{:S(2)}) copy-start(u32[32]{0:T(128)} %constant.81) | copy-start | bytes 388
  7.2 51.4 %copy-start.7 = (s32[1,256]{1,0:T(1,128)S(1)}, s32[1,256]{1,0:T(1,128)}, u32[]{:S(2)}) copy-start(s32[1,256]{1,0:T(1,128)} %param.19) | copy-start | bytes 3076
  7.2 572.1 %reduce-scatter.2.cloned.1.call-start = ((), (), s32[]{:S(2)}) async-start(), calls=%async_computation.2 | async-start | bytes 9437184 | tf_op jit(solution)/shard_map/reduce_scatter | solution.py:178
  10.4 4.1 collective-permute-start.1
  14.6 33.3 %collective-permute-start.2 = (bf16[2,512,512]{1,2,0:T(8,128)(2,1)S(1)}, bf16[2,512,512]{1,2,0:T(8,128)(2,1)S(1)}, u32[]{:S(2)}, u32[]{:S(2)}) collective-permute-start(bf16[2,512,512]{1,2,0:T(8,128)(2,1)S(1)} %maximum_maximum_fusion.1), channel_id=1, source_target_pairs={{0,2},{1,3},{2,4},{3,5},{4,6},{5,7},{8,10},{9,11},{10,12},{11,13},... | collective-permute-start | bytes 3145736 | tf_op jit(solution)/shard_map/ppermute | solution.py:33
  47.9 1.0 copy-start.2
  50.5 123.1 %collective-permute-start.3 = (bf16[2,1024,512]{1,2,0:T(8,128)(2,1)}, bf16[2,1024,512]{1,2,0:T(8,128)(2,1)}, u32[]{:S(2)}, u32[]{:S(2)}) collective-permute-start(bf16[2,1024,512]{1,2,0:T(8,128)(2,1)} %maximum_maximum_fusion), channel_id=1, source_target_pairs={{0,4},{1,5},{2,6},{3,7},{8,12},{9,13},{10,14},{11,15},{16,20},{17,... | collective-permute-start | bytes 6291464 | tf_op jit(solution)/shard_map/ppermute | solution.py:33
  57.1 115.3 %collective-permute-start = (bf16[2,256,512]{1,2,0:T(8,128)(2,1)}, bf16[2,256,512]{1,2,0:T(8,128)(2,1)}, u32[]{:S(2)}, u32[]{:S(2)}) collective-permute-start(bf16[2,256,512]{1,2,0:T(8,128)(2,1)} %pad_maximum_fusion.1), channel_id=1, source_target_pairs={} | collective-permute-start | bytes 1572872 | tf_op jit(solution)/shard_map/ppermute | solution.py:33
  172.4 3.0 copy-start.3
  194.4 3.5 copy-start.5
  200.4 1.0 copy-start.6
  224.5 3.5 copy-start.5
  230.6 1.0 copy-start.6
  254.7 3.6 copy-start.5
  260.8 1.0 copy-start.6
  284.8 3.5 copy-start.5
  290.9 1.0 copy-start.6
  309.8 11.8 %slice-start = ((s8[4718592]{0:T(1024)(128)(4,1)}), s8[524288]{0:T(1024)(128)(4,1)S(1)}, s32[]{:S(2)}) async-start(s8[4718592]{0:T(1024)(128)(4,1)} %bitcast.170), calls=%async_computation.4 | async-start | bytes 1048576
  316.4 5.2 slice-start.1
  344.1 6.7 copy-start.1
  346.9 91.5 %collective-permute-start.5 = (f32[2,1024,512]{2,1,0:T(8,128)S(1)}, f32[2,1024,512]{2,1,0:T(8,128)}, u32[]{:S(2)}, u32[]{:S(2)}) collective-permute-start(f32[2,1024,512]{2,1,0:T(8,128)S(1)} %slice.82), channel_id=1, source_target_pairs={{4,0},{5,1},{6,2},{7,3},{12,8},{13,9},{14,10},{15,11},{20,16},{21,... | collective-permute-start | bytes 12582920 | tf_op jit(solution)/shard_map/ppermute | solution.py:33
  349.8 1.9 collective-permute-start.4
  441.8 45.2 %collective-permute-start.6 = (f32[2,512,512]{2,1,0:T(8,128)S(1)}, f32[2,512,512]{2,1,0:T(8,128)S(1)}, u32[]{:S(2)}, u32[]{:S(2)}) collective-permute-start(f32[2,512,512]{2,1,0:T(8,128)S(1)} %slice.84), channel_id=1, source_target_pairs={{2,0},{3,1},{4,2},{5,3},{6,4},{7,5},{10,8},{11,9},{12,10},{13,11},... | collective-permute-start | bytes 6291464 | tf_op jit(solution)/shard_map/ppermute | solution.py:33
  487.6 4.6 collective-permute-start.7
  492.4 0.8 copy-start.4
  497.8 120.0 %all-gather.4.cloned.1.call-start = ((), (), s32[]{:S(2)}) async-start(), calls=%async_computation.1 | async-start | bytes 4718592 | tf_op jit(solution)/shard_map/all_gather | solution.py:174
  498.5 173.5 %all-reduce.8.cloned.1.call-start = ((), (), s32[]{:S(2)}) async-start(), calls=%async_computation.3 | async-start | bytes 2097152 | tf_op jit(solution)/shard_map/psum | solution.py:184
Sparse Core Ops, SparseCore 0:
  497.9 81.3 reduce-scatter.1
  581.1 36.5 all-gather.3
  620.1 51.8 all-reduce.7
where the time goes:
time: 683 us; the launch traced here: 681 us
  waiting for transfers between devices  321 us (47%)
  local copies, waits for them, and re-layouts  117 us (17%)
  matrix products  116 us (17%)
  loops' own time  40.9 us (6%)
  blocking collectives  31.2 us (5%)
  starting transfers between devices  27.3 us (4%)
  between operations  16.6 us (2%)
  other arithmetic  11.1 us (2%)
    ppermute x8, waiting for transfers between devices, passed_along(): return lax.ppermute(block, axis, route)  157 us
    reduce_scatter x1, waiting for transfers between devices, on_device(): lax.psum_scatter(jnp.einsum('tr,tk->rk', input_rows, value_delta, preferr...  80.7 us
    psum x1, waiting for transfers between devices, on_device(): weight_grad = lax.psum(weight_share, 'dp')  49.4 us
    another operation x1, loops' own time, carried_in(): return lax.fori_loop(0, peers, turn, start)  40.7 us
    sub x4, matrix products, attend_group(): exp_score = jnp.exp(scores - row_max)  33.5 us
    all_gather x1, waiting for transfers between devices, on_device(): lax.all_gather(value_weight, 'ctx', axis=0, tiled=True)  33.2 us
    all_gather x1, blocking collectives, carried_in(): everything = jax.tree.map(lambda part: lax.all_gather(part, axis), value)  31.2 us
    dot_general x4, matrix products, attend_group(): jnp.einsum('gqk,gqd->kd', prob_low, grad_group, preferred_element_type=jn...  27.2 us
  transfers between devices with their start and end apart: 11, of which 8 were waited for; matrix products, arithmetic and copies ran while one was open for 8% of the time, Pallas kernels for 0%

commit v1 on v0

--- a/solution.py
+++ b/solution.py
@@ -181,7 +181,7 @@
         scatter_dimension=0,
         tiled=True,
     )
-    weight_grad = lax.psum(weight_share, "dp")
+    weight_grad = jnp.sum(lax.all_gather(weight_share, "dp"), axis=0)
     return (query_grad, key_grad, input_grad, weight_grad)
 
 

time: 683 us -> 725 us (1.061)
  waiting for transfers between devices: 321 us -> 349 us
    all_gather x0 -> x1, waiting for transfers between devices: none -> 77.5 us  [on_device(): weight_grad = jnp.sum(lax.all_gather(weight_share, 'dp'), axis=0)]
    psum x1 -> x0, waiting for transfers between devices: 49.4 us -> none  [on_device(): weight_grad = lax.psum(weight_share, 'dp')]
  transfers between devices with their start and end apart: 11 -> 11, of which waited for: 8 -> 8; matrix products, arithmetic and copies ran while one was open for 8% -> 7% of each run, Pallas kernels for 0% -> 0%
where the time goes in v1:
time: 725 us; the launch traced here: 720 us
  waiting for transfers between devices  349 us (48%)
  local copies, waits for them, and re-layouts  121 us (17%)
  matrix products  116 us (16%)
  loops' own time  41.5 us (6%)
  blocking collectives  31.2 us (4%)
  starting transfers between devices  27.2 us (4%)
  between operations  16.8 us (2%)
  other arithmetic  15.8 us (2%)
    ppermute x8, waiting for transfers between devices, passed_along(): return lax.ppermute(block, axis, route)  157 us
    reduce_scatter x1, waiting for transfers between devices, on_device(): lax.psum_scatter(jnp.einsum('tr,tk->rk', input_rows, value_delta, preferr...  80.6 us
    all_gather x1, waiting for transfers between devices, on_device(): weight_grad = jnp.sum(lax.all_gather(weight_share, 'dp'), axis=0)  77.5 us
    another operation x1, loops' own time, carried_in(): return lax.fori_loop(0, peers, turn, start)  40.7 us
    sub x4, matrix products, attend_group(): exp_score = jnp.exp(scores - row_max)  33.5 us
    all_gather x1, waiting for transfers between devices, on_device(): lax.all_gather(value_weight, 'ctx', axis=0, tiled=True)  33.2 us
    all_gather x1, blocking collectives, carried_in(): everything = jax.tree.map(lambda part: lax.all_gather(part, axis), value)  31.2 us
    dot_general x4, matrix products, attend_group(): jnp.einsum('gqk,gqd->kd', prob_low, grad_group, preferred_element_type=jn...  27.2 us
  transfers between devices with their start and end apart: 11, of which 8 were waited for; matrix products, arithmetic and copies ran while one was open for 7% of the time, Pallas kernels for 0%

profile of v1, /device:TPU:0, one launch (start us, length us, event | category | flops | bytes accessed | tf_op | source)
XLA Modules:
  0.0 719.5 jit_solution(216528119444521224)
XLA Ops:
  10.4 2.4 collective-permute-start.1
  14.6 11.5 %collective-permute-start.2 = (bf16[2,512,512]{1,2,0:T(8,128)(2,1)S(1)}, bf16[2,512,512]{1,2,0:T(8,128)(2,1)S(1)}, u32[]{:S(2)}, u32[]{:S(2)}) collective-permute-start(bf16[2,512,512]{1,2,0:T(8,128)(2,1)S(1)} %maximum_maximum_fusion.1), channel_id=1, source_target_pairs={{0,2},{1,3},{2,4},{3,5},{4,6},{5,7},{8,10},{9,11},{10,12},{11,13},... | collective-permute-start | bytes 3145736 | tf_op jit(solution)/shard_map/ppermute | solution.py:33
  26.1 21.7 %collective-permute-done.2 = bf16[2,512,512]{1,2,0:T(8,128)(2,1)S(1)} collective-permute-done((bf16[2,512,512]{1,2,0:T(8,128)(2,1)S(1)}, bf16[2,512,512]{1,2,0:T(8,128)(2,1)S(1)}, u32[]{:S(2)}, u32[]{:S(2)}) %collective-permute-start.2) | collective-permute-done | bytes 1048608 | tf_op jit(solution)/shard_map/ppermute | solution.py:33
  50.5 6.7 collective-permute-start.3
  67.4 31.2 %all-reduce.5 = (s32[8]{0:T(128)S(1)}, s32[8]{0:T(128)S(1)}, s32[8]{0:T(128)S(1)}, s32[8]{0:T(128)S(1)}, s32[8]{0:T(128)S(1)}) all-reduce(s32[8]{0:T(128)S(1)} %bitcast_dynamic-update-slice_fusion.1, s32[8]{0:T(128)S(1)} %dynamic-update-slice.1, s32[8]{0:T(128)S(1)} %dynamic-update-slice.2, ...), channel_id=2, replica_groups=mesh['dp'=4,'ctx'=8] {'ctx'}, use_global_device_ids=true, to_apply=%add | all-reduce | flops 40 | bytes 320 | tf_op jit(solution)/shard_map/all_gather | solution.py:15
  98.6 66.3 %while.32 = (s32[]{:T(128)}, s32[]{:T(128)}, s32[]{:T(128)}, s32[]{:T(128)}, s32[]{:T(128)}, /*index=5*/s32[8]{0:T(128)S(1)}, s32[8]{0:T(128)S(1)}, s32[8]{0:T(1...) while((s32[]{:T(128)}, s32[]{:T(128)}, s32[]{:T(128)}, s32[]{:T(128)}, ...), condition=%wide.region_2.3_spmd, body=%wide.region_1.2_spmd.sunk | while | flops 18 | bytes 363 | solution.py:27
  165.6 2.3 copy.53
  167.9 2.3 copy.54
  175.6 2.5 fusion.83
  178.1 121.3 %while.33 = (s32[]{:T(128)}, bf16[4,4,256,128]{3,2,1,0:T(8,128)(2,1)}, f32[4,2304,128]{2,1,0:T(8,128)}, f32[4,2304,128]{2,1,0:T(8,128)}, bf16[4,4,256,128]{2,3,1...) while((s32[]{:T(128)}, ...), condition=%wide.region_7.8_spmd.clone, body=%wide.region_3.7_spmd.clone.sunk | while | flops 3658453504 | bytes 52402368 | solution.py:87
  181.0 8.4 %fusion.118 = (f32[4,256]{1,0:T(4,128)S(1)}, f32[4,256,2304]{2,1,0:T(8,128)}) fusion(pred[256,2304]{1,0:T(8,128)(4,1)S(1)} %compare_and_fusion.2, bf16[4,2304,128]{1,2,0:T(8,128)(2,1)} %get-tuple-element.595, s32[]{:T(128)} %get-tuple-element.576, bf16[4,4,256,128]{2,3,1,0:T(8,128)(2,1)} %get-tuple-element.594), kind=kOutput, calls=%fused_computation.87.clone.1 | convolution fusion | flops 613419264 | bytes 10884096 | tf_op jit(solution)/shard_map/while/body/eval_jaxpr/sub | solution.py:63
  189.4 5.4 multiply_convert_fusion.2
  194.8 3.5 fusion.120
  198.4 2.5 fusion.119
  201.9 6.8 fusion.121
  211.1 8.4 %fusion.118 = (f32[4,256]{1,0:T(4,128)S(1)}, f32[4,256,2304]{2,1,0:T(8,128)}) fusion(pred[256,2304]{1,0:T(8,128)(4,1)S(1)} %compare_and_fusion.2, bf16[4,2304,128]{1,2,0:T(8,128)(2,1)} %get-tuple-element.595, s32[]{:T(128)} %get-tuple-element.576, bf16[4,4,256,128]{2,3,1,0:T(8,128)(2,1)} %get-tuple-element.594), kind=kOutput, calls=%fused_computation.87.clone.1 | convolution fusion | flops 613419264 | bytes 10884096 | tf_op jit(solution)/shard_map/while/body/eval_jaxpr/sub | solution.py:63
  219.5 5.4 multiply_convert_fusion.2
  225.0 3.5 fusion.120
  228.5 2.5 fusion.119
  232.0 6.8 fusion.121
  241.3 8.4 %fusion.118 = (f32[4,256]{1,0:T(4,128)S(1)}, f32[4,256,2304]{2,1,0:T(8,128)}) fusion(pred[256,2304]{1,0:T(8,128)(4,1)S(1)} %compare_and_fusion.2, bf16[4,2304,128]{1,2,0:T(8,128)(2,1)} %get-tuple-element.595, s32[]{:T(128)} %get-tuple-element.576, bf16[4,4,256,128]{2,3,1,0:T(8,128)(2,1)} %get-tuple-element.594), kind=kOutput, calls=%fused_computation.87.clone.1 | convolution fusion | flops 613419264 | bytes 10884096 | tf_op jit(solution)/shard_map/while/body/eval_jaxpr/sub | solution.py:63
  249.7 5.4 multiply_convert_fusion.2
  255.1 3.6 fusion.120
  258.7 2.5 fusion.119
  262.2 6.8 fusion.121
  271.5 8.4 %fusion.118 = (f32[4,256]{1,0:T(4,128)S(1)}, f32[4,256,2304]{2,1,0:T(8,128)}) fusion(pred[256,2304]{1,0:T(8,128)(4,1)S(1)} %compare_and_fusion.2, bf16[4,2304,128]{1,2,0:T(8,128)(2,1)} %get-tuple-element.595, s32[]{:T(128)} %get-tuple-element.576, bf16[4,4,256,128]{2,3,1,0:T(8,128)(2,1)} %get-tuple-element.594), kind=kOutput, calls=%fused_computation.87.clone.1 | convolution fusion | flops 613419264 | bytes 10884096 | tf_op jit(solution)/shard_map/while/body/eval_jaxpr/sub | solution.py:63
  279.9 5.4 multiply_convert_fusion.2
  285.3 3.5 fusion.120
  288.8 2.5 fusion.119
  292.3 6.8 fusion.121
  299.3 11.1 %copy.61 = f32[2304,4,128]{2,1,0:T(4,128)} copy(f32[2304,4,128]{2,0,1:T(8,128)} %bitcast.171) | data formatting | bytes 9437184 | tf_op jit(solution)/shard_map/transpose | solution.py:157
  310.5 6.6 stack_reshape.6
  317.1 5.2 constant_dynamic-update-slice_fusion.6
  322.2 10.9 %copy.62 = f32[2304,4,128]{2,1,0:T(4,128)} copy(f32[2304,4,128]{2,0,1:T(8,128)S(1)} %bitcast.174) | data formatting | bytes 9437184 | tf_op jit(solution)/shard_map/transpose | solution.py:158
  333.1 6.5 stack_reshape.7
  339.7 5.0 constant_dynamic-update-slice_fusion.5
  344.7 2.8 slice.82
  352.4 86.7 %collective-permute-done.5 = f32[2,1024,512]{2,1,0:T(8,128)} collective-permute-done((f32[2,1024,512]{2,1,0:T(8,128)S(1)}, f32[2,1024,512]{2,1,0:T(8,128)}, u32[]{:S(2)}, u32[]{:S(2)}) %collective-permute-start.5) | collective-permute-done | bytes 4194336 | tf_op jit(solution)/shard_map/ppermute | solution.py:33
  439.1 3.2 fusion.73
  443.8 44.0 %collective-permute-done.6 = f32[2,512,512]{2,1,0:T(8,128)S(1)} collective-permute-done((f32[2,512,512]{2,1,0:T(8,128)S(1)}, f32[2,512,512]{2,1,0:T(8,128)S(1)}, u32[]{:S(2)}, u32[]{:S(2)}) %collective-permute-start.6) | collective-permute-done | bytes 2097184 | tf_op jit(solution)/shard_map/ppermute | solution.py:33
  489.6 3.3 collective-permute-done.7
  493.9 4.5 convolution_bitcast_fusion.1
  499.2 80.6 %reduce-scatter.2.cloned.1.call-done = f32[512,512]{0,1:T(8,128)} async-done(((f32[4096,512]{0,1:T(8,128)}), f32[512,512]{0,1:T(8,128)}) %reduce-scatter.2.cloned.1.call-update) | async-done | bytes 1048592 | tf_op jit(solution)/shard_map/reduce_scatter | solution.py:178
  585.2 33.2 %all-gather.6.cloned.1.call-done = bf16[4096,512]{1,0:T(8,128)(2,1)} async-done(((bf16[512,512]{1,0:T(8,128)(2,1)}), bf16[4096,512]{1,0:T(8,128)(2,1)}) %all-gather.6.cloned.1.call-update) | async-done | bytes 4194320 | tf_op jit(solution)/shard_map/all_gather | solution.py:174
  618.4 4.9 fusion.72
  623.3 77.5 %all-gather.8.cloned.1.call-done = f32[2048,512]{0,1:T(8,128)} async-done(((f32[512,512]{0,1:T(8,128)}), f32[2048,512]{0,1:T(8,128)}) %all-gather.8.cloned.1.call-update) | async-done | bytes 4194320 | tf_op jit(solution)/shard_map/all_gather | solution.py:184
  700.7 6.1 reshape.60
  706.8 4.7 reduce_sum.37
  (152 shorter events, 77.2 us)
Async XLA Ops:
  7.2 486.7 %copy-start = (bf16[1,256,4096]{2,1,0:T(8,128)(2,1)S(1)}, bf16[1,256,4096]{2,1,0:T(8,128)(2,1)}, u32[]{:S(2)}) copy-start(bf16[1,256,4096]{2,1,0:T(8,128)(2,1)} %param.12) | copy-start | bytes 6291460
  7.2 54.1 %copy-start.8 = (u32[32]{0:T(128)S(1)}, u32[32]{0:T(128)}, u32[]{:S(2)}) copy-start(u32[32]{0:T(128)} %constant.82) | copy-start | bytes 388
  7.2 51.4 %copy-start.7 = (s32[1,256]{1,0:T(1,128)S(1)}, s32[1,256]{1,0:T(1,128)}, u32[]{:S(2)}) copy-start(s32[1,256]{1,0:T(1,128)} %param.19) | copy-start | bytes 3076
  7.2 572.7 %reduce-scatter.2.cloned.1.call-start = ((), (), s32[]{:S(2)}) async-start(), calls=%async_computation.2 | async-start | bytes 9437184 | tf_op jit(solution)/shard_map/reduce_scatter | solution.py:178
  10.4 4.1 collective-permute-start.1
  14.6 33.3 %collective-permute-start.2 = (bf16[2,512,512]{1,2,0:T(8,128)(2,1)S(1)}, bf16[2,512,512]{1,2,0:T(8,128)(2,1)S(1)}, u32[]{:S(2)}, u32[]{:S(2)}) collective-permute-start(bf16[2,512,512]{1,2,0:T(8,128)(2,1)S(1)} %maximum_maximum_fusion.1), channel_id=1, source_target_pairs={{0,2},{1,3},{2,4},{3,5},{4,6},{5,7},{8,10},{9,11},{10,12},{11,13},... | collective-permute-start | bytes 3145736 | tf_op jit(solution)/shard_map/ppermute | solution.py:33
  47.9 1.0 copy-start.2
  50.5 123.1 %collective-permute-start.3 = (bf16[2,1024,512]{1,2,0:T(8,128)(2,1)}, bf16[2,1024,512]{1,2,0:T(8,128)(2,1)}, u32[]{:S(2)}, u32[]{:S(2)}) collective-permute-start(bf16[2,1024,512]{1,2,0:T(8,128)(2,1)} %maximum_maximum_fusion), channel_id=1, source_target_pairs={{0,4},{1,5},{2,6},{3,7},{8,12},{9,13},{10,14},{11,15},{16,20},{17,... | collective-permute-start | bytes 6291464 | tf_op jit(solution)/shard_map/ppermute | solution.py:33
  57.1 115.3 %collective-permute-start = (bf16[2,256,512]{1,2,0:T(8,128)(2,1)}, bf16[2,256,512]{1,2,0:T(8,128)(2,1)}, u32[]{:S(2)}, u32[]{:S(2)}) collective-permute-start(bf16[2,256,512]{1,2,0:T(8,128)(2,1)} %pad_maximum_fusion.1), channel_id=1, source_target_pairs={} | collective-permute-start | bytes 1572872 | tf_op jit(solution)/shard_map/ppermute | solution.py:33
  172.4 3.0 copy-start.3
  194.8 3.5 copy-start.5
  200.9 1.0 copy-start.6
  225.0 3.5 copy-start.5
  231.0 1.0 copy-start.6
  255.1 3.6 copy-start.5
  261.2 1.0 copy-start.6
  285.3 3.5 copy-start.5
  291.4 1.0 copy-start.6
  310.4 11.8 %slice-start = ((s8[4718592]{0:T(1024)(128)(4,1)}), s8[524288]{0:T(1024)(128)(4,1)S(1)}, s32[]{:S(2)}) async-start(s8[4718592]{0:T(1024)(128)(4,1)} %bitcast.172), calls=%async_computation.4 | async-start | bytes 1048576
  317.1 5.2 slice-start.1
  344.7 6.6 copy-start.1
  347.5 91.6 %collective-permute-start.5 = (f32[2,1024,512]{2,1,0:T(8,128)S(1)}, f32[2,1024,512]{2,1,0:T(8,128)}, u32[]{:S(2)}, u32[]{:S(2)}) collective-permute-start(f32[2,1024,512]{2,1,0:T(8,128)S(1)} %slice.82), channel_id=1, source_target_pairs={{4,0},{5,1},{6,2},{7,3},{12,8},{13,9},{14,10},{15,11},{20,16},{21,... | collective-permute-start | bytes 12582920 | tf_op jit(solution)/shard_map/ppermute | solution.py:33
  350.4 1.8 collective-permute-start.4
  442.5 45.3 %collective-permute-start.6 = (f32[2,512,512]{2,1,0:T(8,128)S(1)}, f32[2,512,512]{2,1,0:T(8,128)S(1)}, u32[]{:S(2)}, u32[]{:S(2)}) collective-permute-start(f32[2,512,512]{2,1,0:T(8,128)S(1)} %slice.84), channel_id=1, source_target_pairs={{2,0},{3,1},{4,2},{5,3},{6,4},{7,5},{10,8},{11,9},{12,10},{13,11},... | collective-permute-start | bytes 6291464 | tf_op jit(solution)/shard_map/ppermute | solution.py:33
  488.3 4.6 collective-permute-start.7
  493.1 0.8 copy-start.4
  498.4 120.0 %all-gather.6.cloned.1.call-start = ((), (), s32[]{:S(2)}) async-start(), calls=%async_computation.1 | async-start | bytes 4718592 | tf_op jit(solution)/shard_map/all_gather | solution.py:174
  499.2 201.6 %all-gather.8.cloned.1.call-start = ((), (), s32[]{:S(2)}) async-start(), calls=%async_computation.3 | async-start | bytes 5242880 | tf_op jit(solution)/shard_map/all_gather | solution.py:184
Sparse Core Ops, SparseCore 0:
  498.5 81.2 reduce-scatter.1
  581.8 36.5 all-gather.5
  620.0 80.7 all-gather.7
